TPU v7x, 32 devices: a whole 2x2x4 slice. The times are simulated.
32 devices in a mesh: wide: 8 (over z, x), narrow: 4 (over y, core).
Axes of the slice: x: 2, y: 2, z: 4, core: 2. Of those that a mesh axis runs over, the one named last changes fastest.
Arguments:
- tokens: bfloat16 [16384, 768], P(('wide', 'narrow')), may hold values from -6 to 6
- timestep: int32 [16], P('wide'), may hold values from 0 to 999
- token_mask: int32 [16384], P(('wide', 'narrow')), may hold values 0 or 1
- time_table: float32 [1000, 128], replicated, may hold values from -6 to 6
- w_ada: bfloat16 [128, 4608], replicated, may hold values from -0.5 to 0.5
- b_ada: float32 [4608], replicated, may hold values from -3 to 3
- gain_one: float32 [768], replicated, may hold values from 0.5 to 1.5
- w_qkv: bfloat16 [3, 768, 768], P(None, None, 'narrow'), may hold values from -0.21875 to 0.21875
- w_out: bfloat16 [768, 768], P('narrow'), may hold values from -3.5 to 3.5
- gain_two: float32 [768], replicated, may hold values from 0.5 to 1.5
- w_up: bfloat16 [768, 3072], P(None, 'narrow'), may hold values from -0.21875 to 0.21875
- b_up: float32 [3072], P('narrow'), may hold values from -3 to 3
- w_down: bfloat16 [3072, 768], P('narrow'), may hold values from -0.109375 to 0.109375
- b_down: float32 [768], replicated, may hold values from -3 to 3
- cotangent: bfloat16 [16384, 768], P(('wide', 'narrow')), may hold values from -6 to 6
Outputs:
- mixed: bfloat16 [16384, 768], P(('wide', 'narrow'))
- grad_tokens: float32 [16384, 768], P(('wide', 'narrow'))
- grad_time_table: float32 [1000, 128], replicated
- grad_w_ada: float32 [128, 4608], replicated
- grad_b_ada: float32 [4608], replicated
- grad_gain_one: float32 [768], replicated
- grad_w_qkv: float32 [3, 768, 768], P(None, None, 'narrow')
- grad_w_out: float32 [768, 768], P('narrow')
- grad_gain_two: float32 [768], replicated
- grad_w_up: float32 [768, 3072], P(None, 'narrow')
- grad_b_up: float32 [3072], P('narrow')
- grad_w_down: float32 [3072, 768], P('narrow')
- grad_b_down: float32 [768], replicated
Inputs may be any that keep to these rules, and one draw needn't show every extreme that they name: One timestep for each sequence of 1024 tokens.
All inputs are finite; a program needn't handle non-finite values. No bound on the sum of `token_mask` on one device may be relied on, other than what follows from the above.
Results may differ from a plain program's by a relative error of at most 0.02.
The roundings to bfloat16 on the way count: a program that leaves them out, or rounds other values in their place, can miss the bound.
Values may be sent and summed in bfloat16 or wider, within the bound.
A program may use at most 192 MiB of HBM per device.

v0:
```python
from functools import partial
import math
import jax
import jax.numpy as jnp
from jax import lax
from jax.sharding import PartitionSpec as P

D = 768
HD = 64
LEN = 1024
SEQS = 2
norm_eps = 1e-06
highest = lax.Precision.HIGHEST


def layer_norm(values, norm_gain):
    centered = values - jnp.mean(values, axis=-1, keepdims=True)
    variance = jnp.mean(centered * centered, axis=-1, keepdims=True)
    return centered * lax.rsqrt(variance + norm_eps) * norm_gain


def norm_back(values, norm_gain, grad_norm):
    _, pullback = jax.vjp(layer_norm, values, norm_gain)
    return pullback(grad_norm)


def rope_tables():
    half_width = HD // 2
    frequency = 10000.0 ** (-2.0 * jnp.arange(half_width, dtype=jnp.float32) / HD)
    angles = jnp.arange(LEN, dtype=jnp.float32)[:, None] * frequency[None, :]
    cos_table = jnp.concatenate([jnp.cos(angles), jnp.cos(angles)], axis=1)[:, None, :]
    sin_table = jnp.concatenate([jnp.sin(angles), jnp.sin(angles)], axis=1)[:, None, :]
    return (cos_table, sin_table)


def rotate(values, cos_table, sin_table):
    half_width = values.shape[-1] // 2
    turned = jnp.concatenate([-values[..., half_width:], values[..., :half_width]], axis=-1)
    return values * cos_table + turned * sin_table


def attend(q_low, k_low, v_low):
    scale_factor = 1.0 / math.sqrt(HD)
    block_rows = min(512, LEN)

    def one_sequence(pieces):
        q_seq, k_seq, v_seq = pieces
        outputs = []
        log_parts = []
        for first_row in range(0, LEN, block_rows):
            scores = (
                jnp.einsum(
                    "qhe,khe->hqk",
                    q_seq[first_row : first_row + block_rows],
                    k_seq,
                    preferred_element_type=jnp.float32,
                )
                * scale_factor
            )
            row_max = jnp.max(scores, axis=-1, keepdims=True)
            exp_scores = jnp.exp(scores - row_max)
            row_sum = jnp.sum(exp_scores, axis=-1, keepdims=True)
            probs_low = (exp_scores / row_sum).astype(jnp.bfloat16)
            outputs.append(
                jnp.einsum("hqk,khe->qhe", probs_low, v_seq, preferred_element_type=jnp.float32)
            )
            log_parts.append((row_max + jnp.log(row_sum))[..., 0])
        return (jnp.concatenate(outputs, axis=0), jnp.concatenate(log_parts, axis=1))

    return lax.map(one_sequence, (q_low, k_low, v_low))


def attend_back(q_low, k_low, v_low, log_sums, grad_heads):
    scale_factor = 1.0 / math.sqrt(HD)
    block_rows = min(512, LEN)

    def one_sequence(pieces):
        q_seq, k_seq, v_seq, sums_seq, grad_seq = pieces
        grad_keys = jnp.zeros(k_seq.shape, jnp.float32)
        grad_values = jnp.zeros(v_seq.shape, jnp.float32)
        grad_queries = []
        for first_row in range(0, LEN, block_rows):
            q_block = q_seq[first_row : first_row + block_rows]
            grad_block = grad_seq[first_row : first_row + block_rows]
            scores = (
                jnp.einsum("qhe,khe->hqk", q_block, k_seq, preferred_element_type=jnp.float32)
                * scale_factor
            )
            probs = jnp.exp(scores - sums_seq[:, first_row : first_row + block_rows, None])
            probs_low = probs.astype(jnp.bfloat16)
            grad_values = grad_values + jnp.einsum(
                "hqk,qhe->khe", probs_low, grad_block, preferred_element_type=jnp.float32
            )
            grad_probs = jnp.einsum(
                "qhe,khe->hqk", grad_block, v_seq, preferred_element_type=jnp.float32
            )
            inner_sum = jnp.sum(probs * grad_probs, axis=-1, keepdims=True)
            grad_scores = (probs * (grad_probs - inner_sum) * scale_factor).astype(jnp.bfloat16)
            grad_queries.append(
                jnp.einsum("hqk,khe->qhe", grad_scores, k_seq, preferred_element_type=jnp.float32)
            )
            grad_keys = grad_keys + jnp.einsum(
                "hqk,qhe->khe", grad_scores, q_block, preferred_element_type=jnp.float32
            )
        return (jnp.concatenate(grad_queries, axis=0), grad_keys, grad_values)

    return lax.map(one_sequence, (q_low, k_low, v_low, log_sums, grad_heads))


def forward(
    tokens,
    timestep,
    time_table,
    w_ada,
    b_ada,
    gain_one,
    w_qkv,
    w_out,
    gain_two,
    w_up,
    b_up,
    w_down,
    b_down,
):
    tok_rows = tokens.shape[0]
    group_heads = w_qkv.shape[2] // HD
    step_pick = (
        timestep[:, None] == jnp.arange(time_table.shape[0], dtype=jnp.int32)[None, :]
    ).astype(jnp.float32)
    picked = jnp.dot(step_pick, time_table, precision=highest)
    cond_low = jax.nn.silu(picked).astype(jnp.bfloat16)
    modulation = jnp.dot(cond_low, w_ada, preferred_element_type=jnp.float32) + b_ada
    positions = lax.axis_index("narrow") * tok_rows + jnp.arange(tok_rows, dtype=jnp.int32)
    row_pick = (positions[:, None] // LEN == jnp.arange(SEQS, dtype=jnp.int32)[None, :]).astype(
        jnp.float32
    )
    mod_tok = jnp.dot(row_pick, modulation, precision=highest).reshape(tok_rows, 6, D)
    residual_in = tokens.astype(jnp.float32)
    norm_one = layer_norm(residual_in, gain_one)
    normed_low = (norm_one * (1.0 + mod_tok[:, 1]) + mod_tok[:, 0]).astype(jnp.bfloat16)
    normed_all = lax.all_gather(normed_low, "narrow", axis=0, tiled=True)
    projected = jnp.einsum("td,kde->kte", normed_all, w_qkv, preferred_element_type=jnp.float32)
    shaped = projected.reshape(3, SEQS, LEN, group_heads, HD)
    cos_table, sin_table = rope_tables()
    q_low = rotate(shaped[0], cos_table, sin_table).astype(jnp.bfloat16)
    k_low = rotate(shaped[1], cos_table, sin_table).astype(jnp.bfloat16)
    v_low = shaped[2].astype(jnp.bfloat16)
    head_out, log_sums = attend(q_low, k_low, v_low)
    heads_low = head_out.astype(jnp.bfloat16).reshape(SEQS * LEN, group_heads * HD)
    attn_part = lax.psum_scatter(
        jnp.dot(
            lax.slice_in_dim(heads_low, 0, tok_rows * lax.axis_size("narrow"), axis=0),
            w_out,
            preferred_element_type=jnp.float32,
        ).astype(jnp.bfloat16),
        "narrow",
        scatter_dimension=0,
        tiled=True,
    ).astype(jnp.float32)
    mid_residual = residual_in + mod_tok[:, 2] * attn_part
    norm_two = layer_norm(mid_residual, gain_two)
    normed_two_low = (norm_two * (1.0 + mod_tok[:, 4]) + mod_tok[:, 3]).astype(jnp.bfloat16)
    normed_two_all = lax.all_gather(normed_two_low, "narrow", axis=0, tiled=True)
    pre_act = jnp.dot(normed_two_all, w_up, preferred_element_type=jnp.float32) + b_up
    act_low = jax.nn.gelu(pre_act, approximate=True).astype(jnp.bfloat16)
    branch = (
        lax.psum_scatter(
            jnp.dot(
                lax.slice_in_dim(act_low, 0, tok_rows * lax.axis_size("narrow"), axis=0),
                w_down,
                preferred_element_type=jnp.float32,
            ).astype(jnp.bfloat16),
            "narrow",
            scatter_dimension=0,
            tiled=True,
        ).astype(jnp.float32)
        + b_down
    )
    mixed = mid_residual + mod_tok[:, 5] * branch
    return (
        mixed,
        step_pick,
        picked,
        cond_low,
        row_pick,
        mod_tok,
        residual_in,
        norm_one,
        normed_all,
        q_low,
        k_low,
        v_low,
        log_sums,
        heads_low,
        attn_part,
        mid_residual,
        norm_two,
        normed_two_all,
        pre_act,
        act_low,
        branch,
    )


def body(
    tokens,
    timestep,
    token_mask,
    time_table,
    w_ada,
    b_ada,
    gain_one,
    w_qkv,
    w_out,
    gain_two,
    w_up,
    b_up,
    w_down,
    b_down,
    cotangent,
):
    weights = (
        time_table,
        w_ada,
        b_ada,
        gain_one,
        w_qkv,
        w_out,
        gain_two,
        w_up,
        b_up,
        w_down,
        b_down,
    )
    saved = forward(tokens, timestep, *weights)
    (
        mixed,
        step_pick,
        picked,
        cond_low,
        row_pick,
        mod_tok,
        residual_in,
        norm_one,
        normed_all,
        q_low,
        k_low,
        v_low,
        log_sums,
        heads_low,
        attn_part,
        mid_residual,
        norm_two,
        normed_two_all,
        pre_act,
        act_low,
        branch,
    ) = saved
    tok_rows = tokens.shape[0]
    group_heads = w_qkv.shape[2] // HD
    grad_mixed = cotangent.astype(jnp.float32) * token_mask.astype(jnp.float32)[:, None]
    grad_gate_two = grad_mixed * branch
    grad_branch = grad_mixed * mod_tok[:, 5]
    b_down_part = jnp.sum(grad_branch, axis=0)
    branch_all = lax.all_gather(grad_branch.astype(jnp.bfloat16), "narrow", axis=0, tiled=True)
    grad_w_down = jnp.einsum("tf,td->fd", act_low, branch_all, preferred_element_type=jnp.float32)
    grad_act = jnp.einsum("td,fd->tf", branch_all, w_down, preferred_element_type=jnp.float32)
    _, gelu_pull = jax.vjp(partial(jax.nn.gelu, approximate=True), pre_act)
    grad_pre_low = gelu_pull(grad_act)[0].astype(jnp.bfloat16)
    grad_b_up = jnp.sum(grad_pre_low, axis=0, dtype=jnp.float32)
    grad_w_up = jnp.einsum(
        "td,tf->df", normed_two_all, grad_pre_low, preferred_element_type=jnp.float32
    )
    grad_normed_two = lax.psum_scatter(
        jnp.einsum(
            "tf,df->td",
            lax.slice_in_dim(grad_pre_low, 0, tok_rows * lax.axis_size("narrow"), axis=0),
            w_up,
            preferred_element_type=jnp.float32,
        ).astype(jnp.bfloat16),
        "narrow",
        scatter_dimension=0,
        tiled=True,
    ).astype(jnp.float32)
    grad_res_two, gain_two_part = norm_back(
        mid_residual, gain_two, grad_normed_two * (1.0 + mod_tok[:, 4])
    )
    grad_mid = grad_mixed + grad_res_two
    grad_gate_one = grad_mid * attn_part
    attention_all = lax.all_gather(
        (grad_mid * mod_tok[:, 2]).astype(jnp.bfloat16), "narrow", axis=0, tiled=True
    )
    grad_w_out = jnp.einsum(
        "te,td->ed", heads_low, attention_all, preferred_element_type=jnp.float32
    )
    grad_heads = jnp.einsum("td,ed->te", attention_all, w_out, preferred_element_type=jnp.float32)
    grad_heads = grad_heads.astype(jnp.bfloat16).reshape(SEQS, LEN, group_heads, HD)
    grad_queries, grad_keys, grad_values = attend_back(q_low, k_low, v_low, log_sums, grad_heads)
    cos_table, sin_table = rope_tables()
    _, rope_pull = jax.vjp(lambda values: rotate(values, cos_table, sin_table), grad_queries)
    grad_projected = jnp.stack([rope_pull(grad_queries)[0], rope_pull(grad_keys)[0], grad_values])
    grad_projected = grad_projected.reshape(3, SEQS * LEN, group_heads * HD).astype(jnp.bfloat16)
    grad_w_qkv = jnp.einsum(
        "td,kte->kde", normed_all, grad_projected, preferred_element_type=jnp.float32
    )
    grad_normed = lax.psum_scatter(
        jnp.einsum("kte,kde->td", grad_projected, w_qkv, preferred_element_type=jnp.float32).astype(
            jnp.bfloat16
        ),
        "narrow",
        scatter_dimension=0,
        tiled=True,
    ).astype(jnp.float32)
    grad_res_one, gain_one_part = norm_back(
        residual_in, gain_one, grad_normed * (1.0 + mod_tok[:, 1])
    )
    grad_tokens = grad_mid + grad_res_one
    grad_mod_flat = jnp.stack(
        [
            grad_normed,
            grad_normed * norm_one,
            grad_gate_one,
            grad_normed_two,
            grad_normed_two * norm_two,
            grad_gate_two,
        ],
        axis=1,
    ).reshape(tok_rows, 6 * D)
    mod_part = jnp.einsum("ts,tm->sm", row_pick, grad_mod_flat, precision=highest)
    grad_modulation, grad_gain_one, grad_gain_two, grad_b_down = (
        lax.psum(mod_part.astype(jnp.bfloat16), "narrow").astype(jnp.float32),
        lax.psum(gain_one_part.astype(jnp.bfloat16), "narrow").astype(jnp.float32),
        lax.psum(gain_two_part.astype(jnp.bfloat16), "narrow").astype(jnp.float32),
        lax.psum(b_down_part.astype(jnp.bfloat16), "narrow").astype(jnp.float32),
    )
    all_modulation = lax.all_gather(grad_modulation, "wide", axis=0, tiled=True)
    all_steps = lax.all_gather(timestep, "wide", axis=0, tiled=True)
    all_pick = (
        all_steps[:, None] == jnp.arange(time_table.shape[0], dtype=jnp.int32)[None, :]
    ).astype(jnp.float32)
    all_picked = jnp.dot(all_pick, time_table, precision=highest)
    all_cond = jax.nn.silu(all_picked).astype(jnp.bfloat16)
    grad_b_ada = jnp.sum(all_modulation, axis=0)
    modulation_low = all_modulation.astype(jnp.bfloat16)
    grad_w_ada = jnp.einsum(
        "sc,sm->cm", all_cond, modulation_low, preferred_element_type=jnp.float32
    )
    grad_condition = jnp.einsum(
        "sm,cm->sc", modulation_low, w_ada, preferred_element_type=jnp.float32
    )
    _, silu_pull = jax.vjp(jax.nn.silu, all_picked)
    grad_time_table = jnp.einsum(
        "sn,sc->nc", all_pick, silu_pull(grad_condition)[0], precision=highest
    )

    def reduce_low(values):
        return lax.psum(values.astype(jnp.bfloat16), "wide").astype(jnp.float32)

    grad_gain_one = reduce_low(grad_gain_one)
    grad_gain_two = reduce_low(grad_gain_two)
    grad_b_up = reduce_low(grad_b_up)
    grad_b_down = reduce_low(grad_b_down)
    grad_w_qkv = reduce_low(grad_w_qkv)
    grad_w_out = reduce_low(grad_w_out)
    grad_w_up = reduce_low(grad_w_up)
    grad_w_down = reduce_low(grad_w_down)
    return (
        mixed.astype(jnp.bfloat16),
        grad_tokens,
        grad_time_table,
        grad_w_ada,
        grad_b_ada,
        grad_gain_one,
        grad_w_qkv,
        grad_w_out,
        grad_gain_two,
        grad_w_up,
        grad_b_up,
        grad_w_down,
        grad_b_down,
    )


def solution(mesh):
    return jax.shard_map(
        body,
        mesh=mesh,
        in_specs=(
            P(("wide", "narrow"), None),
            P("wide"),
            P(("wide", "narrow")),
            P(),
            P(),
            P(),
            P(),
            P(None, None, "narrow"),
            P("narrow", None),
            P(),
            P(None, "narrow"),
            P("narrow"),
            P("narrow", None),
            P(),
            P(("wide", "narrow"), None),
        ),
        out_specs=(
            P(("wide", "narrow"), None),
            P(("wide", "narrow"), None),
            P(),
            P(),
            P(),
            P(),
            P(None, None, "narrow"),
            P("narrow", None),
            P(),
            P(None, "narrow"),
            P("narrow"),
            P("narrow", None),
            P(),
        ),
        check_vma=False,
    )
```

profile of v0, /device:TPU:0, one launch (start us, length us, event | category | flops | bytes accessed | tf_op | source)
XLA Modules:
  0.0 828.8 jit_solution(5324140804440143015)
XLA Ops:
  32.8 27.8 %all-gather.6.cloned.1.call-done = bf16[2048,768]{1,0:T(8,128)(2,1)} async-done(((bf16[512,768]{1,0:T(8,128)(2,1)}), bf16[2048,768]{1,0:T(8,128)(2,1)}) %all-gather.6.cloned.1.call-update) | async-done | bytes 3145744 | tf_op jit(solution)/shard_map/all_gather | solution.py:141
  81.2 20.5 %while.28 = (s32[]{:T(128)}, bf16[2,1024,3,64]{1,3,2,0:T(8,128)(2,1)}, f32[2,3,1024]{2,1,0:T(4,128)}, bf16[2,1024,3,64]{1,3,2,0:T(8,128)(2,1)S(1)}, bf16[2,1024,...) while((s32[]{:T(128)}, bf16[2,1024,3,64]{1,3,2,0:T(8,128)(2,1)}, ...), condition=%wide.region_7.8_spmd.clone, body=%wide.region_2.7_spmd.sunk.clone | while | flops 834404352 | bytes 47524568 | solution.py:70
  115.9 30.3 %reduce-scatter.5.cloned.1.call-done = bf16[512,768]{1,0:T(8,128)(2,1)} async-done(((bf16[2048,768]{1,0:T(8,128)(2,1)}), bf16[512,768]{1,0:T(8,128)(2,1)}) %reduce-scatter.5.cloned.1.call-update) | async-done | bytes 786448 | tf_op jit(solution)/shard_map/reduce_scatter | solution.py:150
  150.8 28.2 %all-gather.8.cloned.1.call-done = bf16[2048,768]{1,0:T(8,128)(2,1)} async-done(((bf16[512,768]{1,0:T(8,128)(2,1)}), bf16[2048,768]{1,0:T(8,128)(2,1)}) %all-gather.8.cloned.1.call-update) | async-done | bytes 3145744 | tf_op jit(solution)/shard_map/all_gather | solution.py:163
  179.0 4.9 fusion.228
  186.6 5.4 convolution_convert_fusion.2
  195.8 34.3 %reduce-scatter.7.cloned.1.call-done = bf16[512,768]{1,0:T(8,128)(2,1)} async-done(((bf16[2048,768]{1,0:T(8,128)(2,1)}), bf16[512,768]{1,0:T(8,128)(2,1)}) %reduce-scatter.7.cloned.1.call-update) | async-done | bytes 786448 | tf_op jit(solution)/shard_map/reduce_scatter | solution.py:167
  234.3 28.6 %all-gather.10.cloned.1.call-done = bf16[2048,768]{1,0:T(8,128)(2,1)} async-done(((bf16[512,768]{1,0:T(8,128)(2,1)}), bf16[2048,768]{1,0:T(8,128)(2,1)}) %all-gather.10.cloned.1.call-update) | async-done | bytes 3145744 | tf_op jit(solution)/shard_map/all_gather | solution.py:265
  262.9 10.9 %fusion.215 = (bf16[768]{0:T(1024)(128)(2,1)}, bf16[2048,768]{1,0:T(8,128)(2,1)S(1)}) fusion(f32[2048,768]{1,0:T(8,128)} %copy-done.93, f32[768]{0:T(1024)} %param.30, bf16[2048,768]{1,0:T(8,128)(2,1)} %all-gather.10.cloned.1.call-done, bf16[768,768]{1,0:T(8,128)(2,1)S(1)} %copy-done), kind=kOutput, calls=%fused_computation.265 | convolution fusion | flops 2450521344 | bytes 13767168 | tf_op jit(solution)/shard_map/td,fd->tf/dot_general | solution.py:267
  279.6 38.1 %reduce-scatter.9.cloned.1.call-done = bf16[512,768]{1,0:T(8,128)(2,1)} async-done(((bf16[2048,768]{1,0:T(8,128)(2,1)}), bf16[512,768]{1,0:T(8,128)(2,1)}) %reduce-scatter.9.cloned.1.call-update) | async-done | bytes 786448 | tf_op jit(solution)/shard_map/reduce_scatter | solution.py:274
  324.1 6.7 convolution_convert_fusion.6
  330.8 7.9 convolution_convert_fusion.5
  338.7 13.8 %all-gather.12.cloned.1.call-done = bf16[2048,768]{1,0:T(8,128)(2,1)} async-done(((bf16[512,768]{1,0:T(8,128)(2,1)}), bf16[2048,768]{1,0:T(8,128)(2,1)}) %all-gather.12.cloned.1.call-update) | async-done | bytes 3145744 | tf_op jit(solution)/shard_map/all_gather | solution.py:290
  360.3 149.5 %while.29 = (s32[]{:T(128)}, f32[2,1024,3,64]{1,3,2,0:T(8,128)}, f32[2,1024,3,64]{1,3,2,0:T(8,128)}, bf16[2,1024,3,64]{1,3,2,0:T(8,128)(2,1)}, bf16[2,1024,3,64]...) while((s32[]{:T(128)}, f32[2,1024,3,64]{1,3,2,0:T(8,128)}, ...), condition=%wide.region_18.19_spmd.clone, body=%wide.region_15.18_spmd.sunk.clone | while | flops 2079926272 | bytes 209329936 | solution.py:107
  372.9 14.0 %fusion.347 = f32[512,3,64]{0,2,1:T(8,128)S(1)} fusion(f32[3,512,1024]{2,1,0:T(8,128)} %fusion.344, f32[3,512,1024]{2,1,0:T(8,128)} %copy-done.2, f32[3,512]{1,0:T(4,128)S(1)} %get-tuple-element.382, bf16[2,1024,3,64]{1,3,2,0:T(8,128)(2,1)S(1)} %get-tuple-element.436, s32[]{:T(128)S(6)} %copy.116), kind=kOutput, calls=%fused_computation.72.clone.1.clone | convolution fusion | flops 215484928 | bytes 25968644 | tf_op jit(solution)/shard_map/while/body/eval_jaxpr/hqk,khe->qhe/dot_general | solution.py:100
  386.9 4.6 fusion.348
  391.5 14.2 %fusion.350 = f32[512,3,64]{0,2,1:T(8,128)S(1)} fusion(f32[3,512,1024]{2,1,0:T(8,128)} %fusion.348, f32[3,512,1024]{2,1,0:T(8,128)} %copy-done.3, f32[3,512]{1,0:T(4,128)S(1)} %get-tuple-element.383, bf16[2,1024,3,64]{1,3,2,0:T(8,128)(2,1)S(1)} %get-tuple-element.436, s32[]{:T(128)S(6)} %copy.116), kind=kOutput, calls=%fused_computation.73.clone.1.clone | convolution fusion | flops 215484928 | bytes 25968644 | tf_op jit(solution)/shard_map/while/body/eval_jaxpr/hqk,khe->qhe/dot_general | solution.py:100
  405.7 14.1 %fusion.352 = f32[3,64,1024]{2,1,0:T(8,128)} fusion(f32[3,512,1024]{2,1,0:T(8,128)} %fusion.348, f32[3,512,1024]{2,1,0:T(8,128)} %copy-done.3, f32[3,512]{1,0:T(4,128)S(1)} %get-tuple-element.383, bf16[2,1024,3,64]{1,3,2,0:T(8,128)(2,1)S(1)} %get-tuple-element.437, s32[]{:T(128)S(6)} %copy.116), kind=kOutput, calls=%fused_computation.47.clone.1.clone | convolution fusion | flops 215484928 | bytes 26165252 | tf_op jit(solution)/shard_map/while/body/eval_jaxpr/hqk,qhe->khe/dot_general | solution.py:102
  419.8 14.3 %fusion.353 = f32[2,1024,3,64]{1,3,2,0:T(8,128)} fusion(f32[2,1024,3,64]{1,3,2,0:T(8,128)} %get-tuple-element.425, s32[]{:T(128)S(6)} %copy.116, f32[3,64,1024]{2,1,0:T(8,128)} %fusion.352, f32[3,512,1024]{2,1,0:T(8,128)} %fusion.344, f32[3,512,1024]{2,1,0:T(8,128)} %copy-done.2, f32[3,512]{1,0:T(4,128)S(1)} %get-tuple-element.382, ...), kind=kOutput, calls=%fused_computation.71.clone.1.clone | convolution fusion | flops 215681536 | bytes 26953216 | tf_op jit(solution)/shard_map/while/body/eval_jaxpr/hqk,qhe->khe/dot_general | solution.py:102
  447.3 14.0 %fusion.347 = f32[512,3,64]{0,2,1:T(8,128)S(1)} fusion(f32[3,512,1024]{2,1,0:T(8,128)} %fusion.344, f32[3,512,1024]{2,1,0:T(8,128)} %copy-done.2, f32[3,512]{1,0:T(4,128)S(1)} %get-tuple-element.382, bf16[2,1024,3,64]{1,3,2,0:T(8,128)(2,1)S(1)} %get-tuple-element.436, s32[]{:T(128)S(6)} %copy.116), kind=kOutput, calls=%fused_computation.72.clone.1.clone | convolution fusion | flops 215484928 | bytes 25968644 | tf_op jit(solution)/shard_map/while/body/eval_jaxpr/hqk,khe->qhe/dot_general | solution.py:100
  461.3 4.6 fusion.348
  465.9 14.2 %fusion.350 = f32[512,3,64]{0,2,1:T(8,128)S(1)} fusion(f32[3,512,1024]{2,1,0:T(8,128)} %fusion.348, f32[3,512,1024]{2,1,0:T(8,128)} %copy-done.3, f32[3,512]{1,0:T(4,128)S(1)} %get-tuple-element.383, bf16[2,1024,3,64]{1,3,2,0:T(8,128)(2,1)S(1)} %get-tuple-element.436, s32[]{:T(128)S(6)} %copy.116), kind=kOutput, calls=%fused_computation.73.clone.1.clone | convolution fusion | flops 215484928 | bytes 25968644 | tf_op jit(solution)/shard_map/while/body/eval_jaxpr/hqk,khe->qhe/dot_general | solution.py:100
  480.1 14.1 %fusion.352 = f32[3,64,1024]{2,1,0:T(8,128)} fusion(f32[3,512,1024]{2,1,0:T(8,128)} %fusion.348, f32[3,512,1024]{2,1,0:T(8,128)} %copy-done.3, f32[3,512]{1,0:T(4,128)S(1)} %get-tuple-element.383, bf16[2,1024,3,64]{1,3,2,0:T(8,128)(2,1)S(1)} %get-tuple-element.437, s32[]{:T(128)S(6)} %copy.116), kind=kOutput, calls=%fused_computation.47.clone.1.clone | convolution fusion | flops 215484928 | bytes 26165252 | tf_op jit(solution)/shard_map/while/body/eval_jaxpr/hqk,qhe->khe/dot_general | solution.py:102
  494.2 14.3 %fusion.353 = f32[2,1024,3,64]{1,3,2,0:T(8,128)} fusion(f32[2,1024,3,64]{1,3,2,0:T(8,128)} %get-tuple-element.425, s32[]{:T(128)S(6)} %copy.116, f32[3,64,1024]{2,1,0:T(8,128)} %fusion.352, f32[3,512,1024]{2,1,0:T(8,128)} %fusion.344, f32[3,512,1024]{2,1,0:T(8,128)} %copy-done.2, f32[3,512]{1,0:T(4,128)S(1)} %get-tuple-element.382, ...), kind=kOutput, calls=%fused_computation.71.clone.1.clone | convolution fusion | flops 215681536 | bytes 26953216 | tf_op jit(solution)/shard_map/while/body/eval_jaxpr/hqk,qhe->khe/dot_general | solution.py:102
  535.2 13.0 %all-reduce.4 = s32[16]{0:T(128)S(1)} all-reduce(s32[16]{0:T(128)S(1)} %dynamic-update-slice), channel_id=1, replica_groups=mesh['wide'=8,'narrow'=4] {'wide'}, use_global_device_ids=true, to_apply=%add.4 | all-reduce | flops 16 | bytes 128
  548.5 119.4 %all-reduce.10.cloned.1.call-done = (bf16[3,768,192]{1,2,0:T(8,128)(2,1)}, bf16[192,768]{1,0:T(8,128)(2,1)}, bf16[768,768]{1,0:T(8,128)(2,1)}, bf16[768,768]{1,0:T(8,128)(2,1)}) async-done(((bf16[3,768,192]{1,2,0:T(8,128)(2,1)}, bf16[192,768]{1,0:T(8,128)(2,1)}, bf16[768,768]{1,0:T(8,128)(2,1)}, bf16[768,768]{1,0:T(8,128)(2,1)}), (bf16[3,768,192]{1,2,0:T(8,128)(2,1)}, bf16[192,768]{1,0:T(8,128)(2,1)}, ...) | async-done | bytes 3538960 | tf_op jit(solution)/shard_map/psum | solution.py:357
  675.6 31.7 %reduce-scatter.11.cloned.1.call-done = bf16[512,768]{1,0:T(8,128)(2,1)} async-done(((bf16[2048,768]{1,0:T(8,128)(2,1)}), bf16[512,768]{1,0:T(8,128)(2,1)}) %reduce-scatter.11.cloned.1.call-update) | async-done | bytes 786448 | tf_op jit(solution)/shard_map/reduce_scatter | solution.py:306
  721.2 9.6 %copy.87 = f32[512,6,768]{0,2,1:T(8,128)} copy(f32[512,6,768]{2,0,1:T(8,128)} %bitcast_dynamic-update-slice_fusion) | data formatting | bytes 18874368 | tf_op jit(solution)/shard_map/stack | solution.py:318
  730.8 8.8 %convolution_convert_fusion = bf16[2,4608]{1,0:T(2,128)(2,1)} fusion(f32[512,4608]{0,1:T(8,128)} %bitcast.318, s32[512]{0:T(512)S(1)} %copy-done.56), kind=kOutput, calls=%fused_computation.129 | convolution fusion | flops 56634368 | bytes 9457664 | tf_op jit(solution)/shard_map/ts,tm->sm/dot_general | solution.py:329
  739.6 11.6 %all-reduce.7 = (bf16[2,4608]{1,0:T(2,128)(2,1)}, bf16[768]{0:T(1024)(128)(2,1)}, bf16[768]{0:T(1024)(128)(2,1)}, bf16[768]{0:T(1024)(128)(2,1)}) all-reduce(bf16[2,4608]{1,0:T(2,128)(2,1)} %convolution_convert_fusion, bf16[768]{0:T(1024)(128)(2,1)} %get-tuple-element.147, ...), channel_id=1, replica_groups=mesh['wide'=8,'narrow'=4] {'narrow'}, use_global_device_ids=true, to_apply=%region_22.23 | all-reduce | flops 11520 | bytes 46080 | tf_op jit(solution)/shard_map/psum | solution.py:331
  751.2 22.5 %all-reduce.5 = (bf16[768]{0:T(1024)(128)(2,1)}, bf16[768]{0:T(1024)(128)(2,1)}, bf16[768]{0:T(1024)(128)(2,1)}, bf16[768]{0:T(1024)(128)(2,1)}) all-reduce(bf16[768]{0:T(1024)(128)(2,1)} %get-tuple-element.188, bf16[768]{0:T(1024)(128)(2,1)} %get-tuple-element.189, ...), channel_id=1, replica_groups=mesh['wide'=8,'narrow'=4] {'wide'}, use_global_device_ids=true, to_apply=%region_26.27 | all-reduce | flops 3072 | bytes 12288 | tf_op jit(solution)/shard_map/psum | solution.py:357
  779.5 30.9 %all-gather = f32[8,2,4608]{2,1,0:T(2,128)S(1)} all-gather(f32[1,2,4608]{2,1,0:T(2,128)S(1)} %bitcast_convert_fusion.1), channel_id=1, replica_groups=mesh['wide'=8,'narrow'=4] {'wide'}, dimensions={0}, use_global_device_ids=true | all-gather | bytes 331776 | tf_op jit(solution)/shard_map/all_gather | solution.py:336
  (357 shorter events, 205.3 us)
Async XLA Ops:
  7.2 179.4 %copy-start = (bf16[768,768]{1,0:T(8,128)(2,1)S(1)}, bf16[768,768]{1,0:T(8,128)(2,1)}, u32[]{:S(2)}) copy-start(bf16[768,768]{1,0:T(8,128)(2,1)} %param.31) | copy-start | bytes 3538948
  7.2 53.5 %all-gather.6.cloned.1.call-start = ((), (), s32[]{:S(2)}) async-start(), calls=%async_computation.4 | async-start | bytes 3932160 | tf_op jit(solution)/shard_map/all_gather | solution.py:141
  8.7 17.8 %copy-start.60 = (f32[512]{0:T(512)}, f32[512]{0:T(512)S(1)}, u32[]{:S(2)}) copy-start(f32[512]{0:T(512)S(1)} %broadcast_multiply_fusion.3) | copy-start | bytes 6148
  10.2 16.3 %copy-start.70 = (f32[512]{0:T(512)}, f32[512]{0:T(512)S(1)}, u32[]{:S(2)}) copy-start(f32[512]{0:T(512)S(1)} %fusion.206) | copy-start | bytes 6148
  29.3 31.4 %copy-start.87 = (bf16[3,768,192]{1,2,0:T(8,128)(2,1)S(1)}, bf16[3,768,192]{1,2,0:T(8,128)(2,1)}, u32[]{:S(2)}) copy-start(bf16[3,768,192]{1,2,0:T(8,128)(2,1)} %param.26) | copy-start | bytes 2654212
  29.3 116.8 %reduce-scatter.5.cloned.1.call-start = ((), (), s32[]{:S(2)}) async-start(), calls=%async_computation.5 | async-start | bytes 3932160 | tf_op jit(solution)/shard_map/reduce_scatter | solution.py:150
  108.0 71.0 %all-gather.8.cloned.1.call-start = ((), (), s32[]{:S(2)}) async-start(), calls=%async_computation.6 | async-start | bytes 3932160 | tf_op jit(solution)/shard_map/all_gather | solution.py:163
  115.9 33.0 %copy-start.68 = (f32[768]{0:T(1024)S(1)}, f32[768]{0:T(1024)}, u32[]{:S(2)}) copy-start(f32[768]{0:T(1024)} %param.28) | copy-start | bytes 9220
  148.5 172.2 %copy-start.4 = (f32[512,768]{1,0:T(8,128)}, f32[512,768]{1,0:T(8,128)S(1)}, u32[]{:S(2)}) copy-start(f32[512,768]{1,0:T(8,128)S(1)} %get-tuple-element.198) | copy-start | bytes 4718596
  148.5 172.2 %copy-start.62 = (f32[512]{0:T(512)}, f32[512]{0:T(512)S(1)}, u32[]{:S(2)}) copy-start(f32[512]{0:T(512)S(1)} %broadcast_multiply_fusion.2) | copy-start | bytes 6148
  149.0 171.7 %copy-start.72 = (f32[512]{0:T(512)}, f32[512]{0:T(512)S(1)}, u32[]{:S(2)}) copy-start(f32[512]{0:T(512)S(1)} %fusion.207) | copy-start | bytes 6148
  150.3 79.8 %reduce-scatter.7.cloned.1.call-start = ((), (), s32[]{:S(2)}) async-start(), calls=%async_computation.7 | async-start | bytes 3932160 | tf_op jit(solution)/shard_map/reduce_scatter | solution.py:167
  150.8 35.8 %copy-start.89 = (f32[768]{0:T(1024)S(1)}, f32[768]{0:T(1024)}, u32[]{:S(2)}) copy-start(f32[768]{0:T(1024)} %param.30) | copy-start | bytes 9220
  192.0 70.9 %all-gather.10.cloned.1.call-start = ((), (), s32[]{:S(2)}) async-start(), calls=%async_computation.8 | async-start | bytes 3932160 | tf_op jit(solution)/shard_map/all_gather | solution.py:265
  192.8 128.7 %copy-start.64 = (f32[512]{0:T(512)}, f32[512]{0:T(512)S(1)}, u32[]{:S(2)}) copy-start(f32[512]{0:T(512)S(1)} %convert_element_type.178) | copy-start | bytes 6148
  234.2 83.4 %reduce-scatter.9.cloned.1.call-start = ((), (), s32[]{:S(2)}) async-start(), calls=%async_computation.9 | async-start | bytes 3932160 | tf_op jit(solution)/shard_map/reduce_scatter | solution.py:274
  262.9 12.6 %copy-start.86 = (bf16[768,768]{1,0:T(8,128)(2,1)S(1)}, bf16[768,768]{1,0:T(8,128)(2,1)}, u32[]{:S(2)}) copy-start(bf16[768,768]{1,0:T(8,128)(2,1)} %param.29) | copy-start | bytes 3538948
  279.5 41.1 %copy-start.80 = (f32[512]{0:T(512)S(1)}, f32[512]{0:T(512)}, u32[]{:S(2)}) copy-start(f32[512]{0:T(512)} %copy-done.79) | copy-start | bytes 6148
  279.5 73.1 %all-gather.12.cloned.1.call-start = ((), (), s32[]{:S(2)}) async-start(), calls=%async_computation.10 | async-start | bytes 3932160 | tf_op jit(solution)/shard_map/all_gather | solution.py:290
  323.9 344.0 %all-reduce.10.cloned.1.call-start = ((), (), s32[]{:S(2)}) async-start(), calls=%async_computation.12 | async-start | bytes 7077888 | tf_op jit(solution)/shard_map/psum | solution.py:357
  330.8 21.8 %copy-start.52 = (bf16[192,768]{1,0:T(8,128)(2,1)S(1)}, bf16[192,768]{1,0:T(8,128)(2,1)}, u32[]{:S(2)}) copy-start(bf16[192,768]{1,0:T(8,128)(2,1)} %param.27) | copy-start | bytes 884740
  527.1 180.2 %reduce-scatter.11.cloned.1.call-start = ((), (), s32[]{:S(2)}) async-start(), calls=%async_computation.11 | async-start | bytes 3932160 | tf_op jit(solution)/shard_map/reduce_scatter | solution.py:306
  533.0 15.2 %copy-start.48 = (f32[1000,128]{1,0:T(8,128)S(1)}, f32[1000,128]{1,0:T(8,128)}, u32[]{:S(2)}) copy-start(f32[1000,128]{1,0:T(8,128)} %param.22) | copy-start | bytes 1536004
  548.2 124.2 %copy-start.82 = (s32[16]{0:T(128)}, s32[16]{0:T(128)S(1)}, u32[]{:S(2)}) copy-start(s32[16]{0:T(128)S(1)} %all-reduce.4) | copy-start | bytes 196
  672.4 34.9 %copy-start.7 = (bf16[512,768]{1,0:T(8,128)(2,1)S(1)}, bf16[512,768]{1,0:T(8,128)(2,1)}, u32[]{:S(2)}) copy-start(bf16[512,768]{1,0:T(8,128)(2,1)} %param.19) | copy-start | bytes 2359300
  672.4 34.9 %copy-start.14 = (f32[512,1,768]{2,0,1:T(8,128)S(1)}, f32[512,1,768]{2,0,1:T(8,128)}, u32[]{:S(2)}) copy-start(f32[512,1,768]{2,0,1:T(8,128)} %copy-done.13) | copy-start | bytes 4718596
  672.4 34.9 %copy-start.61 = (f32[512]{0:T(512)S(1)}, f32[512]{0:T(512)}, u32[]{:S(2)}) copy-start(f32[512]{0:T(512)} %copy-done.60) | copy-start | bytes 6148
  672.4 34.9 %copy-start.67 = (f32[768]{0:T(1024)S(1)}, f32[768]{0:T(1024)}, u32[]{:S(2)}) copy-start(f32[768]{0:T(1024)} %param.25) | copy-start | bytes 9220
  672.4 34.9 %copy-start.71 = (f32[512]{0:T(512)S(1)}, f32[512]{0:T(512)}, u32[]{:S(2)}) copy-start(f32[512]{0:T(512)} %copy-done.70) | copy-start | bytes 6148
  674.0 35.8 %copy-start.78 = (f32[512]{0:T(512)S(1)}, f32[512]{0:T(512)}, u32[]{:S(2)}) copy-start(f32[512]{0:T(512)} %copy-done.77) | copy-start | bytes 6148
  730.8 82.6 %copy-start.38 = (bf16[128,4608]{1,0:T(8,128)(2,1)S(1)}, bf16[128,4608]{1,0:T(8,128)(2,1)}, u32[]{:S(2)}) copy-start(bf16[128,4608]{1,0:T(8,128)(2,1)} %param.23) | copy-start | bytes 3538948
  739.6 80.2 %copy-start.76 = (f32[512]{0:T(512)S(1)}, f32[512]{0:T(512)}, u32[]{:S(2)}) copy-start(f32[512]{0:T(512)} %copy-done.74) | copy-start | bytes 6148
  (80 other events, 265.3 us)
Sparse Core Ops, SparseCore 0:
  29.4 31.2 all-gather.5
  108.1 37.9 reduce-scatter.4
  150.4 28.5 all-gather.7
  192.2 37.9 reduce-scatter.6
  234.3 28.5 all-gather.9
  279.6 37.9 reduce-scatter.8
  324.0 28.5 all-gather.11
  527.3 140.5 all-reduce.9
  670.4 36.8 reduce-scatter.10
where the time goes:
time: 836 us; the launch traced here: 829 us
  waiting for transfers between devices  352 us (42%)
  matrix products  232 us (28%)
  local copies, waits for them, and re-layouts  85.4 us (10%)
  blocking collectives  77.9 us (9%)
  other arithmetic  63.3 us (8%)
  between operations  15.6 us (2%)
    psum x1, waiting for transfers between devices, reduce_low(): return lax.psum(values.astype(jnp.bfloat16), 'wide').astype(jnp.float32)  119 us
    dot_general x4, matrix products, one_sequence(): jnp.einsum('hqk,qhe->khe', grad_scores, q_block, preferred_element_type=j...  56.7 us
    dot_general x4, matrix products, one_sequence(): jnp.einsum('hqk,khe->qhe', grad_scores, k_seq, preferred_element_type=jnp...  56.3 us
    reduce_scatter x1, waiting for transfers between devices, body(): lax.psum_scatter(jnp.einsum('tf,df->td', lax.slice_in_dim(grad_pre_low, 0...  38.1 us
    reduce_scatter x1, waiting for transfers between devices, forward(): lax.psum_scatter(jnp.dot(lax.slice_in_dim(act_low, 0, tok_rows * lax.axis...  34.3 us
    unnamed x183, local copies, waits for them, and re-layouts  33.3 us
    reduce_scatter x1, waiting for transfers between devices, body(): lax.psum_scatter(jnp.einsum('kte,kde->td', grad_projected, w_qkv, preferr...  31.7 us
    all_gather x1, blocking collectives, body(): all_modulation = lax.all_gather(grad_modulation, 'wide', axis=0, tiled=True)  30.9 us
  transfers between devices with their start and end apart: 9, of which 9 were waited for; matrix products, arithmetic and copies ran while one was open for 5% of the time, Pallas kernels for 0%

commit v1 on v0

--- a/solution.py
+++ b/solution.py
@@ -333,7 +333,12 @@
         lax.psum(gain_two_part.astype(jnp.bfloat16), "narrow").astype(jnp.float32),
         lax.psum(b_down_part.astype(jnp.bfloat16), "narrow").astype(jnp.float32),
     )
-    all_modulation = lax.all_gather(grad_modulation, "wide", axis=0, tiled=True)
+    ring = [grad_modulation]
+    for hop in range(7):
+        ring.append(lax.ppermute(ring[-1], "wide", [(dev, (dev + 1) % 8) for dev in range(8)]))
+    all_modulation = jnp.roll(
+        jnp.concatenate(ring[::-1], axis=0), (lax.axis_index("wide") + 1) * ring[0].shape[0], axis=0
+    )
     all_steps = lax.all_gather(timestep, "wide", axis=0, tiled=True)
     all_pick = (
         all_steps[:, None] == jnp.arange(time_table.shape[0], dtype=jnp.int32)[None, :]

time: 836 us -> 786 us (0.940)
  blocking collectives: 77.9 us -> 45.4 us
  waiting for transfers between devices: 352 us -> 338 us
    psum x1, waiting for transfers between devices: 119 us -> 79.9 us  [reduce_low(): return lax.psum(values.astype(jnp.bfloat16), 'wide').astype(jnp.float32)]
    all_gather x1 -> x0, blocking collectives: 30.9 us -> none  [body(): all_modulation = lax.all_gather(grad_modulation, 'wide', axis=0, tiled=True)]
    ppermute x0 -> x7, waiting for transfers between devices: none -> 23.6 us  [body(): lax.ppermute(ring[-1], 'wide', [(dev, (dev + 1) % 8) for dev in range(8)])]
    all_gather x1, waiting for transfers between devices: 13.8 us -> 28.6 us  [body(): lax.all_gather((grad_mid * mod_tok[:, 2]).astype(jnp.bfloat16), 'narrow',...]
    reduce_scatter x1, waiting for transfers between devices: 31.7 us -> 18.2 us  [body(): lax.psum_scatter(jnp.einsum('kte,kde->td', grad_projected, w_qkv, preferr...]
    unnamed x183 -> x207, local copies, waits for them, and re-layouts: 33.3 us -> 30.4 us
  transfers between devices with their start and end apart: 9 -> 16, of which waited for: 9 -> 13; matrix products, arithmetic and copies ran while one was open for 5% -> 10% of each run, Pallas kernels for 0% -> 0%
where the time goes in v1:
time: 786 us; the launch traced here: 779 us
  waiting for transfers between devices  338 us (43%)
  matrix products  230 us (29%)
  local copies, waits for them, and re-layouts  83.8 us (11%)
  other arithmetic  58.6 us (7%)
  blocking collectives  45.4 us (6%)
  between operations  15.7 us (2%)
    psum x1, waiting for transfers between devices, reduce_low(): return lax.psum(values.astype(jnp.bfloat16), 'wide').astype(jnp.float32)  79.9 us
    dot_general x4, matrix products, one_sequence(): jnp.einsum('hqk,qhe->khe', grad_scores, q_block, preferred_element_type=j...  57.5 us
    dot_general x4, matrix products, one_sequence(): jnp.einsum('hqk,khe->qhe', grad_scores, k_seq, preferred_element_type=jnp...  55.8 us
    reduce_scatter x1, waiting for transfers between devices, body(): lax.psum_scatter(jnp.einsum('tf,df->td', lax.slice_in_dim(grad_pre_low, 0...  38.1 us
    reduce_scatter x1, waiting for transfers between devices, forward(): lax.psum_scatter(jnp.dot(lax.slice_in_dim(act_low, 0, tok_rows * lax.axis...  34.3 us
    unnamed x207, local copies, waits for them, and re-layouts  30.4 us
    reduce_scatter x1, waiting for transfers between devices, forward(): lax.psum_scatter(jnp.dot(lax.slice_in_dim(heads_low, 0, tok_rows * lax.ax...  30.3 us
    all_gather x1, waiting for transfers between devices, body(): lax.all_gather(grad_branch.astype(jnp.bfloat16), 'narrow', axis=0, tiled=...  28.6 us
  transfers between devices with their start and end apart: 16, of which 13 were waited for; matrix products, arithmetic and copies ran while one was open for 10% of the time, Pallas kernels for 0%

profile of v1, /device:TPU:0, one launch (start us, length us, event | category | flops | bytes accessed | tf_op | source)
XLA Modules:
  0.0 779.1 jit_solution(2683376683679497840)
XLA Ops:
  32.8 27.9 %all-gather.5.cloned.1.call-done = bf16[2048,768]{1,0:T(8,128)(2,1)} async-done(((bf16[512,768]{1,0:T(8,128)(2,1)}), bf16[2048,768]{1,0:T(8,128)(2,1)}) %all-gather.5.cloned.1.call-update) | async-done | bytes 3145744 | tf_op jit(solution)/shard_map/all_gather | solution.py:141
  81.2 20.5 %while.28 = (s32[]{:T(128)}, bf16[2,1024,3,64]{1,3,2,0:T(8,128)(2,1)}, f32[2,3,1024]{2,1,0:T(4,128)}, bf16[2,1024,3,64]{1,3,2,0:T(8,128)(2,1)S(1)}, bf16[2,1024,...) while((s32[]{:T(128)}, bf16[2,1024,3,64]{1,3,2,0:T(8,128)(2,1)}, ...), condition=%wide.region_7.8_spmd.clone, body=%wide.region_2.7_spmd.sunk.clone | while | flops 834404352 | bytes 47524568 | solution.py:70
  115.9 30.3 %reduce-scatter.5.cloned.1.call-done = bf16[512,768]{1,0:T(8,128)(2,1)} async-done(((bf16[2048,768]{1,0:T(8,128)(2,1)}), bf16[512,768]{1,0:T(8,128)(2,1)}) %reduce-scatter.5.cloned.1.call-update) | async-done | bytes 786448 | tf_op jit(solution)/shard_map/reduce_scatter | solution.py:150
  150.9 28.2 %all-gather.7.cloned.1.call-done = bf16[2048,768]{1,0:T(8,128)(2,1)} async-done(((bf16[512,768]{1,0:T(8,128)(2,1)}), bf16[2048,768]{1,0:T(8,128)(2,1)}) %all-gather.7.cloned.1.call-update) | async-done | bytes 3145744 | tf_op jit(solution)/shard_map/all_gather | solution.py:163
  186.6 5.4 convolution_convert_fusion.2
  195.7 34.3 %reduce-scatter.7.cloned.1.call-done = bf16[512,768]{1,0:T(8,128)(2,1)} async-done(((bf16[2048,768]{1,0:T(8,128)(2,1)}), bf16[512,768]{1,0:T(8,128)(2,1)}) %reduce-scatter.7.cloned.1.call-update) | async-done | bytes 786448 | tf_op jit(solution)/shard_map/reduce_scatter | solution.py:167
  234.2 28.6 %all-gather.9.cloned.1.call-done = bf16[2048,768]{1,0:T(8,128)(2,1)} async-done(((bf16[512,768]{1,0:T(8,128)(2,1)}), bf16[2048,768]{1,0:T(8,128)(2,1)}) %all-gather.9.cloned.1.call-update) | async-done | bytes 3145744 | tf_op jit(solution)/shard_map/all_gather | solution.py:265
  262.8 10.9 %fusion.218 = (bf16[768]{0:T(1024)(128)(2,1)}, bf16[2048,768]{1,0:T(8,128)(2,1)S(1)}) fusion(f32[2048,768]{1,0:T(8,128)} %copy-done.105, f32[768]{0:T(1024)} %param.30, bf16[2048,768]{1,0:T(8,128)(2,1)} %all-gather.9.cloned.1.call-done, bf16[768,768]{1,0:T(8,128)(2,1)S(1)} %copy-done), kind=kOutput, calls=%fused_computation.269 | convolution fusion | flops 2450521344 | bytes 13767168 | tf_op jit(solution)/shard_map/td,fd->tf/dot_general | solution.py:267
  279.5 38.1 %reduce-scatter.9.cloned.1.call-done = bf16[512,768]{1,0:T(8,128)(2,1)} async-done(((bf16[2048,768]{1,0:T(8,128)(2,1)}), bf16[512,768]{1,0:T(8,128)(2,1)}) %reduce-scatter.9.cloned.1.call-update) | async-done | bytes 786448 | tf_op jit(solution)/shard_map/reduce_scatter | solution.py:274
  323.9 28.6 %all-gather.11.cloned.1.call-done = bf16[2048,768]{1,0:T(8,128)(2,1)} async-done(((bf16[512,768]{1,0:T(8,128)(2,1)}), bf16[2048,768]{1,0:T(8,128)(2,1)}) %all-gather.11.cloned.1.call-update) | async-done | bytes 3145744 | tf_op jit(solution)/shard_map/all_gather | solution.py:290
  360.2 149.6 %while.29 = (s32[]{:T(128)}, f32[2,1024,3,64]{1,3,2,0:T(8,128)}, f32[2,1024,3,64]{1,3,2,0:T(8,128)}, bf16[2,1024,3,64]{1,3,2,0:T(8,128)(2,1)}, bf16[2,1024,3,64]...) while((s32[]{:T(128)}, f32[2,1024,3,64]{1,3,2,0:T(8,128)}, ...), condition=%wide.region_18.19_spmd.clone, body=%wide.region_15.18_spmd.sunk.clone | while | flops 2079926272 | bytes 209329936 | solution.py:107
  372.8 14.2 %fusion.346 = f32[512,3,64]{0,2,1:T(8,128)S(1)} fusion(f32[3,512,1024]{2,1,0:T(8,128)} %fusion.343, f32[3,512,1024]{2,1,0:T(8,128)} %copy-done.2, f32[3,512]{1,0:T(4,128)S(1)} %get-tuple-element.365, bf16[2,1024,3,64]{1,3,2,0:T(8,128)(2,1)S(1)} %get-tuple-element.419, s32[]{:T(128)S(6)} %copy.95), kind=kOutput, calls=%fused_computation.72.clone.1.clone | convolution fusion | flops 215484928 | bytes 25968644 | tf_op jit(solution)/shard_map/while/body/eval_jaxpr/hqk,khe->qhe/dot_general | solution.py:100
  391.7 13.7 %fusion.349 = f32[512,3,64]{0,2,1:T(8,128)S(1)} fusion(f32[3,512,1024]{2,1,0:T(8,128)} %fusion.347, f32[3,512,1024]{2,1,0:T(8,128)} %copy-done.3, f32[3,512]{1,0:T(4,128)S(1)} %get-tuple-element.366, bf16[2,1024,3,64]{1,3,2,0:T(8,128)(2,1)S(1)} %get-tuple-element.419, s32[]{:T(128)S(6)} %copy.95), kind=kOutput, calls=%fused_computation.73.clone.1.clone | convolution fusion | flops 215484928 | bytes 25968644 | tf_op jit(solution)/shard_map/while/body/eval_jaxpr/hqk,khe->qhe/dot_general | solution.py:100
  405.3 14.1 %fusion.351 = f32[3,64,1024]{2,1,0:T(8,128)} fusion(f32[3,512,1024]{2,1,0:T(8,128)} %fusion.347, f32[3,512,1024]{2,1,0:T(8,128)} %copy-done.3, f32[3,512]{1,0:T(4,128)S(1)} %get-tuple-element.366, bf16[2,1024,3,64]{1,3,2,0:T(8,128)(2,1)S(1)} %get-tuple-element.420, s32[]{:T(128)S(6)} %copy.95), kind=kOutput, calls=%fused_computation.47.clone.1.clone | convolution fusion | flops 215484928 | bytes 26165252 | tf_op jit(solution)/shard_map/while/body/eval_jaxpr/hqk,qhe->khe/dot_general | solution.py:102
  419.4 14.7 %fusion.352 = f32[2,1024,3,64]{1,3,2,0:T(8,128)} fusion(f32[2,1024,3,64]{1,3,2,0:T(8,128)} %get-tuple-element.408, s32[]{:T(128)S(6)} %copy.95, f32[3,64,1024]{2,1,0:T(8,128)} %fusion.351, f32[3,512,1024]{2,1,0:T(8,128)} %fusion.343, f32[3,512,1024]{2,1,0:T(8,128)} %copy-done.2, f32[3,512]{1,0:T(4,128)S(1)} %get-tuple-element.365, ...), kind=kOutput, calls=%fused_computation.71.clone.1.clone | convolution fusion | flops 215681536 | bytes 26953216 | tf_op jit(solution)/shard_map/while/body/eval_jaxpr/hqk,qhe->khe/dot_general | solution.py:102
  447.4 14.2 %fusion.346 = f32[512,3,64]{0,2,1:T(8,128)S(1)} fusion(f32[3,512,1024]{2,1,0:T(8,128)} %fusion.343, f32[3,512,1024]{2,1,0:T(8,128)} %copy-done.2, f32[3,512]{1,0:T(4,128)S(1)} %get-tuple-element.365, bf16[2,1024,3,64]{1,3,2,0:T(8,128)(2,1)S(1)} %get-tuple-element.419, s32[]{:T(128)S(6)} %copy.95), kind=kOutput, calls=%fused_computation.72.clone.1.clone | convolution fusion | flops 215484928 | bytes 25968644 | tf_op jit(solution)/shard_map/while/body/eval_jaxpr/hqk,khe->qhe/dot_general | solution.py:100
  466.3 13.7 %fusion.349 = f32[512,3,64]{0,2,1:T(8,128)S(1)} fusion(f32[3,512,1024]{2,1,0:T(8,128)} %fusion.347, f32[3,512,1024]{2,1,0:T(8,128)} %copy-done.3, f32[3,512]{1,0:T(4,128)S(1)} %get-tuple-element.366, bf16[2,1024,3,64]{1,3,2,0:T(8,128)(2,1)S(1)} %get-tuple-element.419, s32[]{:T(128)S(6)} %copy.95), kind=kOutput, calls=%fused_computation.73.clone.1.clone | convolution fusion | flops 215484928 | bytes 25968644 | tf_op jit(solution)/shard_map/while/body/eval_jaxpr/hqk,khe->qhe/dot_general | solution.py:100
  479.9 14.1 %fusion.351 = f32[3,64,1024]{2,1,0:T(8,128)} fusion(f32[3,512,1024]{2,1,0:T(8,128)} %fusion.347, f32[3,512,1024]{2,1,0:T(8,128)} %copy-done.3, f32[3,512]{1,0:T(4,128)S(1)} %get-tuple-element.366, bf16[2,1024,3,64]{1,3,2,0:T(8,128)(2,1)S(1)} %get-tuple-element.420, s32[]{:T(128)S(6)} %copy.95), kind=kOutput, calls=%fused_computation.47.clone.1.clone | convolution fusion | flops 215484928 | bytes 26165252 | tf_op jit(solution)/shard_map/while/body/eval_jaxpr/hqk,qhe->khe/dot_general | solution.py:102
  494.0 14.7 %fusion.352 = f32[2,1024,3,64]{1,3,2,0:T(8,128)} fusion(f32[2,1024,3,64]{1,3,2,0:T(8,128)} %get-tuple-element.408, s32[]{:T(128)S(6)} %copy.95, f32[3,64,1024]{2,1,0:T(8,128)} %fusion.351, f32[3,512,1024]{2,1,0:T(8,128)} %fusion.343, f32[3,512,1024]{2,1,0:T(8,128)} %copy-done.2, f32[3,512]{1,0:T(4,128)S(1)} %get-tuple-element.365, ...), kind=kOutput, calls=%fused_computation.71.clone.1.clone | convolution fusion | flops 215681536 | bytes 26953216 | tf_op jit(solution)/shard_map/while/body/eval_jaxpr/hqk,qhe->khe/dot_general | solution.py:102
  525.6 6.7 convolution_convert_fusion.6
  532.3 8.1 %convolution_convert_fusion.5 = bf16[768,768]{1,0:T(8,128)(2,1)} fusion(bf16[2048,768]{1,0:T(8,128)(2,1)S(1)} %copy-done.97, f32[2048,768]{1,0:T(8,128)} %copy-done.105, f32[768]{0:T(1024)S(1)} %copy-done.102), kind=kOutput, calls=%fused_computation.195 | convolution fusion | flops 2432237568 | bytes 10619904 | tf_op jit(solution)/shard_map/tf,td->fd/dot_general | solution.py:266
  545.1 18.2 %reduce-scatter.11.cloned.1.call-done = bf16[512,768]{1,0:T(8,128)(2,1)} async-done(((bf16[2048,768]{1,0:T(8,128)(2,1)}), bf16[512,768]{1,0:T(8,128)(2,1)}) %reduce-scatter.11.cloned.1.call-update) | async-done | bytes 786448 | tf_op jit(solution)/shard_map/reduce_scatter | solution.py:306
  574.4 9.9 %copy.66 = f32[512,6,768]{0,2,1:T(8,128)} copy(f32[512,6,768]{2,0,1:T(8,128)} %bitcast_dynamic-update-slice_fusion) | data formatting | bytes 18874368 | tf_op jit(solution)/shard_map/stack | solution.py:318
  586.3 8.2 %convolution_convert_fusion = bf16[2,4608]{1,0:T(2,128)(2,1)S(1)} fusion(f32[512,4608]{0,1:T(8,128)} %bitcast.313, s32[512]{0:T(512)S(1)} %copy-done.55), kind=kOutput, calls=%fused_computation.129 | convolution fusion | flops 56634368 | bytes 9457664 | tf_op jit(solution)/shard_map/ts,tm->sm/dot_general | solution.py:329
  594.5 12.0 %all-reduce.7 = (bf16[2,4608]{1,0:T(2,128)(2,1)S(1)}, bf16[768]{0:T(1024)(128)(2,1)}, bf16[768]{0:T(1024)(128)(2,1)}, bf16[768]{0:T(1024)(128)(2,1)}) all-reduce(bf16[2,4608]{1,0:T(2,128)(2,1)S(1)} %convolution_convert_fusion, bf16[768]{0:T(1024)(128)(2,1)S(1)} %get-tuple-element.132, ...), channel_id=1, replica_groups=mesh['wide'=8,'narrow'=4] {'narrow'}, use_global_device_ids=true, to_apply=%region_22.23 | all-reduce | flops 11520 | bytes 46080 | tf_op jit(solution)/shard_map/psum | solution.py:331
  608.2 6.0 collective-permute-done
  615.7 11.3 %all-reduce.4 = s32[16]{0:T(128)S(1)} all-reduce(s32[16]{0:T(128)S(1)} %dynamic-update-slice), channel_id=1, replica_groups=mesh['wide'=8,'narrow'=4] {'wide'}, use_global_device_ids=true, to_apply=%add.4 | all-reduce | flops 16 | bytes 128
  630.5 79.9 %all-reduce.10.cloned.1.call-done = (bf16[3,768,192]{1,2,0:T(8,128)(2,1)}, bf16[192,768]{1,0:T(8,128)(2,1)}, bf16[768,768]{1,0:T(8,128)(2,1)}, bf16[768,768]{1,0:T(8,128)(2,1)}) async-done(((bf16[3,768,192]{1,2,0:T(8,128)(2,1)}, bf16[192,768]{1,0:T(8,128)(2,1)}, bf16[768,768]{1,0:T(8,128)(2,1)}, bf16[768,768]{1,0:T(8,128)(2,1)}), (bf16[3,768,192]{1,2,0:T(8,128)(2,1)}, bf16[192,768]{1,0:T(8,128)(2,1)}, ...) | async-done | bytes 3538960 | tf_op jit(solution)/shard_map/psum | solution.py:362
  719.6 5.2 collective-permute-done.3
  725.6 5.8 collective-permute-done.4
  731.4 6.6 collective-permute-done.5
  739.7 22.1 %all-reduce.5 = (bf16[768]{0:T(1024)(128)(2,1)S(1)}, bf16[768]{0:T(1024)(128)(2,1)S(1)}, bf16[768]{0:T(1024)(128)(2,1)S(1)}, bf16[768]{0:T(1024)(128)(2,1)S(1)}) all-reduce(bf16[768]{0:T(1024)(128)(2,1)S(1)} %copy-done.92, bf16[768]{0:T(1024)(128)(2,1)S(1)} %copy-done.93, ...), channel_id=1, replica_groups=mesh['wide'=8,'narrow'=4] {'wide'}, use_global_device_ids=true, to_apply=%region_26.27 | all-reduce | flops 3072 | bytes 12288 | tf_op jit(solution)/shard_map/psum | solution.py:362
  (394 shorter events, 217.0 us)
Async XLA Ops:
  7.2 179.4 %copy-start = (bf16[768,768]{1,0:T(8,128)(2,1)S(1)}, bf16[768,768]{1,0:T(8,128)(2,1)}, u32[]{:S(2)}) copy-start(bf16[768,768]{1,0:T(8,128)(2,1)} %param.31) | copy-start | bytes 3538948
  7.2 53.5 %all-gather.5.cloned.1.call-start = ((), (), s32[]{:S(2)}) async-start(), calls=%async_computation.4 | async-start | bytes 3932160 | tf_op jit(solution)/shard_map/all_gather | solution.py:141
  29.2 31.4 %copy-start.99 = (bf16[3,768,192]{1,2,0:T(8,128)(2,1)S(1)}, bf16[3,768,192]{1,2,0:T(8,128)(2,1)}, u32[]{:S(2)}) copy-start(bf16[3,768,192]{1,2,0:T(8,128)(2,1)} %param.26) | copy-start | bytes 2654212
  29.3 116.9 %reduce-scatter.5.cloned.1.call-start = ((), (), s32[]{:S(2)}) async-start(), calls=%async_computation.5 | async-start | bytes 3932160 | tf_op jit(solution)/shard_map/reduce_scatter | solution.py:150
  108.0 71.0 %all-gather.7.cloned.1.call-start = ((), (), s32[]{:S(2)}) async-start(), calls=%async_computation.6 | async-start | bytes 3932160 | tf_op jit(solution)/shard_map/all_gather | solution.py:163
  115.9 33.0 %copy-start.74 = (f32[768]{0:T(1024)S(1)}, f32[768]{0:T(1024)}, u32[]{:S(2)}) copy-start(f32[768]{0:T(1024)} %param.28) | copy-start | bytes 9220
  148.5 172.1 %copy-start.4 = (f32[512,768]{1,0:T(8,128)}, f32[512,768]{1,0:T(8,128)S(1)}, u32[]{:S(2)}) copy-start(f32[512,768]{1,0:T(8,128)S(1)} %get-tuple-element.183) | copy-start | bytes 4718596
  148.5 172.1 %copy-start.68 = (f32[512]{0:T(512)}, f32[512]{0:T(512)S(1)}, u32[]{:S(2)}) copy-start(f32[512]{0:T(512)S(1)} %broadcast_multiply_fusion.2) | copy-start | bytes 6148
  149.0 171.6 %copy-start.78 = (f32[512]{0:T(512)}, f32[512]{0:T(512)S(1)}, u32[]{:S(2)}) copy-start(f32[512]{0:T(512)S(1)} %fusion.208) | copy-start | bytes 6148
  150.3 79.7 %reduce-scatter.7.cloned.1.call-start = ((), (), s32[]{:S(2)}) async-start(), calls=%async_computation.7 | async-start | bytes 3932160 | tf_op jit(solution)/shard_map/reduce_scatter | solution.py:167
  150.9 35.7 %copy-start.101 = (f32[768]{0:T(1024)S(1)}, f32[768]{0:T(1024)}, u32[]{:S(2)}) copy-start(f32[768]{0:T(1024)} %param.30) | copy-start | bytes 9220
  191.9 70.9 %all-gather.9.cloned.1.call-start = ((), (), s32[]{:S(2)}) async-start(), calls=%async_computation.8 | async-start | bytes 3932160 | tf_op jit(solution)/shard_map/all_gather | solution.py:265
  192.7 128.7 %copy-start.70 = (f32[512]{0:T(512)}, f32[512]{0:T(512)S(1)}, u32[]{:S(2)}) copy-start(f32[512]{0:T(512)S(1)} %convert_element_type.178) | copy-start | bytes 6148
  234.1 83.4 %reduce-scatter.9.cloned.1.call-start = ((), (), s32[]{:S(2)}) async-start(), calls=%async_computation.9 | async-start | bytes 3932160 | tf_op jit(solution)/shard_map/reduce_scatter | solution.py:274
  279.4 41.1 %copy-start.85 = (f32[512]{0:T(512)S(1)}, f32[512]{0:T(512)}, u32[]{:S(2)}) copy-start(f32[512]{0:T(512)} %copy-done.84) | copy-start | bytes 6148
  279.4 73.1 %all-gather.11.cloned.1.call-start = ((), (), s32[]{:S(2)}) async-start(), calls=%async_computation.10 | async-start | bytes 3932160 | tf_op jit(solution)/shard_map/all_gather | solution.py:290
  321.4 35.0 %copy-start.80 = (f32[512]{0:T(512)}, f32[512]{0:T(512)S(1)}, u32[]{:S(2)}) copy-start(f32[512]{0:T(512)S(1)} %negate_multiply_fusion.1) | copy-start | bytes 6148
  323.8 239.5 %reduce-scatter.11.cloned.1.call-start = ((), (), s32[]{:S(2)}) async-start(), calls=%async_computation.11 | async-start | bytes 3932160 | tf_op jit(solution)/shard_map/reduce_scatter | solution.py:306
  525.2 185.2 %all-reduce.10.cloned.1.call-start = ((), (), s32[]{:S(2)}) async-start(), calls=%async_computation.12 | async-start | bytes 7077888 | tf_op jit(solution)/shard_map/psum | solution.py:362
  606.5 110.1 %copy-start.59 = (bf16[2,4608]{1,0:T(2,128)(2,1)}, bf16[2,4608]{1,0:T(2,128)(2,1)S(1)}, u32[]{:S(2)}) copy-start(bf16[2,4608]{1,0:T(2,128)(2,1)S(1)} %get-tuple-element.172) | copy-start | bytes 55300
  606.5 7.7 collective-permute-start
  614.2 102.3 %copy-start.60 = (f32[2,4608]{1,0:T(2,128)}, f32[2,4608]{1,0:T(2,128)S(1)}, u32[]{:S(2)}) copy-start(f32[2,4608]{1,0:T(2,128)S(1)} %collective-permute-done) | copy-start | bytes 110596
  614.2 12.8 %collective-permute-start.1 = (f32[2,4608]{1,0:T(2,128)S(1)}, f32[2,4608]{1,0:T(2,128)S(1)}, u32[]{:S(2)}, u32[]{:S(2)}) collective-permute-start(f32[2,4608]{1,0:T(2,128)S(1)} %collective-permute-done), channel_id=1, source_target_pairs={{0,4},{4,8},{8,12},{12,16},{16,20},{20,24},{24,28},{28,0},{1,5},{5... | collective-permute-start | bytes 110600 | tf_op jit(solution)/shard_map/ppermute | solution.py:338
  627.0 87.9 %copy-start.89 = (s32[16]{0:T(128)}, s32[16]{0:T(128)S(1)}, u32[]{:S(2)}) copy-start(s32[16]{0:T(128)S(1)} %all-reduce.4) | copy-start | bytes 196
  627.0 89.5 %copy-start.61 = (f32[2,4608]{1,0:T(2,128)}, f32[2,4608]{1,0:T(2,128)S(1)}, u32[]{:S(2)}) copy-start(f32[2,4608]{1,0:T(2,128)S(1)} %collective-permute-done.1) | copy-start | bytes 110596
  627.0 91.1 %collective-permute-start.2 = (f32[2,4608]{1,0:T(2,128)S(1)}, f32[2,4608]{1,0:T(2,128)S(1)}, u32[]{:S(2)}, u32[]{:S(2)}) collective-permute-start(f32[2,4608]{1,0:T(2,128)S(1)} %collective-permute-done.1), channel_id=1, source_target_pairs={{0,4},{4,8},{8,12},{12,16},{16,20},{20,24},{24,28},{28,0},{1,5},{5... | collective-permute-start | bytes 110600 | tf_op jit(solution)/shard_map/ppermute | solution.py:338
  718.1 6.7 collective-permute-start.3
  724.8 6.7 collective-permute-start.4
  731.4 6.7 collective-permute-start.5
  738.1 26.1 %collective-permute-start.6 = (f32[2,4608]{1,0:T(2,128)S(1)}, f32[2,4608]{1,0:T(2,128)}, u32[]{:S(2)}, u32[]{:S(2)}) collective-permute-start(f32[2,4608]{1,0:T(2,128)S(1)} %collective-permute-done.5), channel_id=1, source_target_pairs={{0,4},{4,8},{8,12},{12,16},{16,20},{20,24},{24,28},{28,0},{1,5},{5... | collective-permute-start | bytes 110600 | tf_op jit(solution)/shard_map/ppermute | solution.py:338
  738.1 34.2 %copy-start.1 = (bf16[768,768]{1,0:T(8,128)(2,1)S(1)}, bf16[768,768]{1,0:T(8,128)(2,1)}, u32[]{:S(2)}) copy-start(bf16[768,768]{1,0:T(8,128)(2,1)} %param.31) | copy-start | bytes 3538948
  739.7 31.2 %copy-start.90 = (s32[16]{0:T(128)S(1)}, s32[16]{0:T(128)}, u32[]{:S(2)}) copy-start(s32[16]{0:T(128)} %copy-done.89) | copy-start | bytes 196
  (99 other events, 759.9 us)
Sparse Core Ops, SparseCore 0:
  29.4 31.2 all-gather.4
  108.1 37.9 reduce-scatter.4
  150.5 28.5 all-gather.6
  192.1 37.9 reduce-scatter.6
  234.2 28.5 all-gather.8
  279.6 37.9 reduce-scatter.8
  323.9 28.5 all-gather.10
  525.3 37.9 reduce-scatter.10
  568.4 141.9 all-reduce.9
